TPU v7x, 128 devices: a whole 4x4x4 slice. The times are simulated.
128 devices in a mesh: blk: 16 (over y, x_hi, core), rep: 8 (over x_lo, z).
Axes of the slice: x: 4 (x_hi: 2, x_lo: 2; x = x_hi * 2 + x_lo), y: 4, z: 4, core: 2. Of those that a mesh axis runs over, the one named last changes fastest.
Arguments:
- cotangent: bfloat16 [512, 256, 128], P('blk', 'rep'), may hold values from -6 to 6
- relu_mask: int32 [512, 256, 128], P('blk', 'rep'), may hold values 0 or 1
- aggregated: bfloat16 [512, 256, 128], P('blk', 'rep'), may hold values from -6 to 6
- weight: bfloat16 [256, 256], P('rep'), may hold values from -0.375 to 0.375
- tiles: bfloat16 [512, 16, 128, 128], P('blk'), may hold values from -0.125 to 0.125
- col_block: int32 [512, 16], P('blk'), may hold values from 0 to 511, as said below
- live_count: int32 [512], P('blk'), may hold values from 1 to 16, as said below
Outputs:
- input_grad: bfloat16 [512, 256, 128], P('blk', 'rep')
- weight_grad: float32 [256, 256], P('rep')
Inputs may be any that keep to these rules, and one draw needn't show every extreme that they name: The slab of a row block b is b // 32; the slab of col_block[b, s] lies at most 2 slabs from it around the closed cycle of the 16 slabs, and both distance 2 directions occur. `live_count`: row blocks of one slab share a density level, so live counts differ from slab to slab; some row block has all 16 slots live.
All inputs are finite; a program needn't handle non-finite values. No bound on the sum of `relu_mask` on one device may be relied on, other than what follows from the above.
Results may differ from a plain program's by a relative error of at most 0.0049.
Values may be sent and summed in bfloat16 or wider, within the bound.
A program may use at most 128 MiB of HBM per device.

v0:
```python
import math
import jax
import jax.numpy as jnp
from jax import lax
from jax.sharding import PartitionSpec as P

REACH = 2


def from_behind(value, axis, steps):
    count = lax.axis_size(axis)
    pairs = [(source, (source + steps) % count) for source in range(count)]
    return lax.ppermute(value, axis, pairs)


def on_device(cotangent, relu_mask, aggregated, weight, tiles, col_block, live_count):
    blocks_here = cotangent.shape[0]
    cols_here = cotangent.shape[1]
    tile_size = cotangent.shape[2]
    grad_z = cotangent * relu_mask.astype(jnp.bfloat16)
    gathered_part = lax.all_gather(grad_z, "rep", axis=1, tiled=True)
    grad_h = jnp.einsum("io,bon->bin", weight, gathered_part, preferred_element_type=jnp.float32)
    col_part = jnp.einsum(
        "bin,bon->io", aggregated, gathered_part, preferred_element_type=jnp.float32
    )
    grad_w = col_part
    grad_h, grad_w = (grad_h, grad_w)
    nodes_all = lax.axis_size("blk") * blocks_here * tile_size
    weight_grad = lax.psum(grad_w, "blk") * (1.0 / math.sqrt(nodes_all))
    grad_hb = grad_h.astype(jnp.bfloat16)
    slot_count = tiles.shape[1]
    slot_ids = jnp.arange(slot_count, dtype=jnp.int32)
    live = (slot_ids[None, :] < live_count[:, None]).astype(jnp.float32).reshape(-1)
    contrib = jnp.einsum("bkij,bfi->bkfj", tiles, grad_hb, preferred_element_type=jnp.float32)
    flat_terms = contrib.reshape(blocks_here * slot_count, cols_here * tile_size)
    targets = col_block.reshape(-1)
    slabs = lax.axis_size("blk")
    own_slab = lax.axis_index("blk")
    target_slab = targets // blocks_here
    window_slot = (target_slab - own_slab + REACH + slabs) % slabs
    position = window_slot * blocks_here + targets % blocks_here
    window_rows = (2 * REACH + 1) * blocks_here
    row_ids = jnp.arange(window_rows, dtype=jnp.int32)
    selector = (position[None, :] == row_ids[:, None]).astype(jnp.float32) * live[None, :]
    window = jnp.dot(
        selector, flat_terms, preferred_element_type=jnp.float32, precision=lax.Precision.HIGHEST
    )
    window = window.reshape(2 * REACH + 1, blocks_here, cols_here, tile_size)
    input_grad = window[REACH]
    upward = window[2 * REACH]
    downward = window[0]
    for step in range(REACH):
        upward = from_behind(upward, "blk", 1)
        downward = from_behind(downward, "blk", -1)
        if step + 1 < REACH:
            upward = upward + window[2 * REACH - step - 1]
            downward = downward + window[step + 1]
    input_grad = input_grad + upward + downward
    return (input_grad.astype(jnp.bfloat16), weight_grad)


def solution(mesh):
    placed = (
        P("blk", "rep", None),
        P("blk", "rep", None),
        P("blk", "rep", None),
        P("rep", None),
        P("blk", None, None, None),
        P("blk", None),
        P("blk"),
    )
    return jax.shard_map(
        on_device,
        mesh=mesh,
        in_specs=placed,
        out_specs=(P("blk", "rep", None), P("rep", None)),
        check_vma=False,
    )
```

profile of v0, /device:TPU:0, one launch (start us, length us, event | category | flops | bytes accessed | tf_op | source)
XLA Modules:
  0.0 174.0 jit_solution(14960853211397327882)
XLA Ops:
  7.2 0.0 copy-start
  7.2 0.0 all-gather.2.cloned.1.call-start
  7.2 1.9 %convert_multiply_fusion = bf16[32,32,128]{2,1,0:T(8,128)(2,1)} fusion(bf16[32,32,128]{2,1,0:T(8,128)(2,1)} %param.7, s32[32,32,128]{2,1,0:T(8,128)} %param.8), kind=kLoop, calls=%fused_computation.19 | loop fusion | flops 262144 | bytes 1048576 | tf_op jit(solution)/shard_map/mul | solution.py:20
  9.1 0.0 all-gather.2.cloned.1.call-update
  9.1 0.8 copy.9
  9.9 0.1 reshape.102
  10.0 0.7 fusion.13
  10.7 0.1 reshape.104
  10.8 43.8 %all-gather.2.cloned.1.call-done = bf16[32,256,128]{2,1,0:T(8,128)(2,1)} async-done(((bf16[32,32,128]{2,1,0:T(8,128)(2,1)}), bf16[32,256,128]{2,1,0:T(8,128)(2,1)}) %all-gather.2.cloned.1.call-update) | async-done | bytes 2097168 | tf_op jit(solution)/shard_map/all_gather | solution.py:21
  54.6 9.9 %fusion.4 = f32[32,32,16,128]{3,1,2,0:T(8,128)} fusion(bf16[32,16,128,128]{3,2,1,0:T(8,128)(2,1)} %param.11, bf16[32,256,128]{2,1,0:T(8,128)(2,1)} %all-gather.2.cloned.1.call-done, bf16[32,256]{1,0:T(8,128)(2,1)} %param.10), kind=kOutput, calls=%fused_computation.6 | convolution fusion | flops 604110848 | bytes 27279360 | tf_op jit(solution)/shard_map/bkij,bfi->bkfj/dot_general | solution.py:34
  64.5 11.3 %fusion = f32[160,4096]{1,0:T(8,128)S(1)} fusion(f32[64,8,32,128]{3,2,1,0:T(8,128)} %bitcast.46, f32[512]{0:T(512)S(1)} %reshape.104, s32[512]{0:T(512)S(1)} %fusion.18), kind=kOutput, calls=%fused_computation | convolution fusion | flops 4026695680 | bytes 11014144 | tf_op jit(solution)/shard_map/dot_general | solution.py:45
  75.9 0.2 slice_bitcast_fusion.4
  76.0 0.1 copy.13
  76.1 0.1 collective-permute-start
  76.2 0.1 copy.15
  76.3 5.4 %collective-permute-start.2 = (f32[32,32,128]{2,1,0:T(8,128)S(1)}, f32[32,32,128]{2,1,0:T(8,128)S(1)}, u32[]{:S(2)}, u32[]{:S(2)}) collective-permute-start(f32[32,32,128]{2,1,0:T(8,128)S(1)} %bitcast.47), channel_id=1, source_target_pairs={{0,120},{8,0},{16,8},{24,16},{32,24},{40,32},{48,40},{56,48},{64,5... | collective-permute-start | bytes 1572872 | tf_op jit(solution)/shard_map/ppermute | solution.py:13
  81.7 0.1 copy.16
  81.8 0.0 copy-start.1
  81.8 0.1 copy.14
  81.9 8.8 %collective-permute-done = f32[32,32,128]{2,1,0:T(8,128)S(1)} collective-permute-done((f32[32,32,128]{2,1,0:T(8,128)S(1)}, f32[32,32,128]{2,1,0:T(8,128)S(1)}, u32[]{:S(2)}, u32[]{:S(2)}) %collective-permute-start) | collective-permute-done | bytes 524320 | tf_op jit(solution)/shard_map/ppermute | solution.py:13
  90.8 0.1 bitcast_add_fusion.1
  90.9 0.1 collective-permute-start.1
  90.9 0.0 collective-permute-done.2
  91.0 0.1 bitcast_add_fusion
  91.0 5.4 %collective-permute-start.3 = (f32[32,32,128]{2,1,0:T(8,128)S(1)}, f32[32,32,128]{2,1,0:T(8,128)S(1)}, u32[]{:S(2)}, u32[]{:S(2)}) collective-permute-start(f32[32,32,128]{2,1,0:T(8,128)S(1)} %bitcast_add_fusion), channel_id=1, source_target_pairs={{0,120},{8,0},{16,8},{24,16},{32,24},{40,32},{48,40},{56,48},{64,5... | collective-permute-start | bytes 1572872 | tf_op jit(solution)/shard_map/ppermute | solution.py:13
  96.4 0.1 copy.12
  96.5 0.0 copy-done
  96.6 0.0 copy-done.1
  96.6 0.7 convolution_bitcast_fusion
  97.3 68.4 %psum.7 = f32[32,256]{1,0:T(8,128)S(1)} all-reduce(f32[32,256]{1,0:T(8,128)S(1)} %convolution_bitcast_fusion), channel_id=1, replica_groups=mesh['blk'=16,'rep'=8] {'blk'}, use_global_device_ids=true, to_apply=%region_0.0 | all-reduce | flops 8192 | bytes 65536 | tf_op jit(solution)/shard_map/psum | solution.py:29
  165.6 0.6 broadcast_multiply_fusion
  166.2 0.0 collective-permute-done.1
  166.2 0.0 collective-permute-done.3
  166.3 0.9 fusion.6
  (1 shorter events, 0.0 us)
Async XLA Ops:
  7.2 89.4 %copy-start = (bf16[32,32,128]{2,1,0:T(8,128)(2,1)S(1)}, bf16[32,32,128]{2,1,0:T(8,128)(2,1)}, u32[]{:S(2)}) copy-start(bf16[32,32,128]{2,1,0:T(8,128)(2,1)} %param.9) | copy-start | bytes 786436
  7.2 47.5 %all-gather.2.cloned.1.call-start = ((), (), s32[]{:S(2)}) async-start(), calls=%async_computation | async-start | bytes 2359296 | tf_op jit(solution)/shard_map/all_gather | solution.py:21
  76.1 14.6 %collective-permute-start = (f32[32,32,128]{2,1,0:T(8,128)S(1)}, f32[32,32,128]{2,1,0:T(8,128)S(1)}, u32[]{:S(2)}, u32[]{:S(2)}) collective-permute-start(f32[32,32,128]{2,1,0:T(8,128)S(1)} %bitcast.48), channel_id=1, source_target_pairs={{0,8},{8,16},{16,24},{24,32},{32,40},{40,48},{48,56},{56,64},{64,7... | collective-permute-start | bytes 1572872 | tf_op jit(solution)/shard_map/ppermute | solution.py:13
  76.3 14.6 %collective-permute-start.2 = (f32[32,32,128]{2,1,0:T(8,128)S(1)}, f32[32,32,128]{2,1,0:T(8,128)S(1)}, u32[]{:S(2)}, u32[]{:S(2)}) collective-permute-start(f32[32,32,128]{2,1,0:T(8,128)S(1)} %bitcast.47), channel_id=1, source_target_pairs={{0,120},{8,0},{16,8},{24,16},{32,24},{40,32},{48,40},{56,48},{64,5... | collective-permute-start | bytes 1572872 | tf_op jit(solution)/shard_map/ppermute | solution.py:13
  81.8 14.7 %copy-start.1 = (bf16[32,256,128]{2,1,0:T(8,128)(2,1)S(1)}, bf16[32,256,128]{2,1,0:T(8,128)(2,1)}, u32[]{:S(2)}) copy-start(bf16[32,256,128]{2,1,0:T(8,128)(2,1)} %all-gather.2.cloned.1.call-done) | copy-start | bytes 6291460
  90.9 75.4 %collective-permute-start.1 = (f32[32,32,128]{2,1,0:T(8,128)S(1)}, f32[32,32,128]{2,1,0:T(8,128)S(1)}, u32[]{:S(2)}, u32[]{:S(2)}) collective-permute-start(f32[32,32,128]{2,1,0:T(8,128)S(1)} %bitcast_add_fusion.1), channel_id=1, source_target_pairs={{0,8},{8,16},{16,24},{24,32},{32,40},{40,48},{48,56},{56,64},{64,7... | collective-permute-start | bytes 1572872 | tf_op jit(solution)/shard_map/ppermute | solution.py:13
  91.0 75.2 %collective-permute-start.3 = (f32[32,32,128]{2,1,0:T(8,128)S(1)}, f32[32,32,128]{2,1,0:T(8,128)S(1)}, u32[]{:S(2)}, u32[]{:S(2)}) collective-permute-start(f32[32,32,128]{2,1,0:T(8,128)S(1)} %bitcast_add_fusion), channel_id=1, source_target_pairs={{0,120},{8,0},{16,8},{24,16},{32,24},{40,32},{48,40},{56,48},{64,5... | collective-permute-start | bytes 1572872 | tf_op jit(solution)/shard_map/ppermute | solution.py:13
Sparse Core Ops, SparseCore 0:
  10.2 44.3 all-gather.1
where the time goes:
time: 174 us
  blocking collectives  68.4 us (39%)
  waiting for transfers between devices  52.7 us (30%)
  matrix products  21.9 us (13%)
  between operations  14.1 us (8%)
  starting transfers between devices  11 us (6%)
  other arithmetic  4.3 us (2%)
    psum x1, blocking collectives, on_device(): weight_grad = lax.psum(grad_w, 'blk') * (1.0 / math.sqrt(nodes_all))  68.4 us
    all_gather x1, waiting for transfers between devices, on_device(): gathered_part = lax.all_gather(grad_z, 'rep', axis=1, tiled=True)  43.8 us
    dot_general x1, matrix products, on_device(): jnp.dot(selector, flat_terms, preferred_element_type=jnp.float32, precisi...  11.3 us
    ppermute x4, starting transfers between devices, from_behind(): return lax.ppermute(value, axis, pairs)  11 us
    dot_general x1, matrix products, on_device(): jnp.einsum('bkij,bfi->bkfj', tiles, grad_hb, preferred_element_type=jnp.f...  9.9 us
    ppermute x4, waiting for transfers between devices, from_behind(): return lax.ppermute(value, axis, pairs)  8.83 us
  transfers between devices with their start and end apart: 5, of which 2 were waited for; matrix products, arithmetic and copies ran while one was open for 2% of the time, Pallas kernels for 0%

commit v1 on v0

--- a/solution.py
+++ b/solution.py
@@ -3,6 +3,7 @@
 import jax.numpy as jnp
 from jax import lax
 from jax.sharding import PartitionSpec as P
+from jax.lax import all_gather
 
 REACH = 2
 
@@ -26,7 +27,7 @@
     grad_w = col_part
     grad_h, grad_w = (grad_h, grad_w)
     nodes_all = lax.axis_size("blk") * blocks_here * tile_size
-    weight_grad = lax.psum(grad_w, "blk") * (1.0 / math.sqrt(nodes_all))
+    weight_grad = jnp.sum(all_gather(grad_w, "blk"), 0) * (1.0 / math.sqrt(nodes_all))
     grad_hb = grad_h.astype(jnp.bfloat16)
     slot_count = tiles.shape[1]
     slot_ids = jnp.arange(slot_count, dtype=jnp.int32)

time: 174 us -> 134 us (0.77)
  blocking collectives: 68.4 us -> 26.7 us
    psum x1 -> x0, blocking collectives: 68.4 us -> none  [on_device(): weight_grad = lax.psum(grad_w, 'blk') * (1.0 / math.sqrt(nodes_all))]
    all_gather x0 -> x1, blocking collectives: none -> 26.7 us  [on_device(): all_gather(grad_w, 'blk')]
  transfers between devices with their start and end apart: 5 -> 5, of which waited for: 2 -> 2; matrix products, arithmetic and copies ran while one was open for 2% -> 3% of each run, Pallas kernels for 0% -> 0%
where the time goes in v1:
time: 134 us; the launch traced here: 132 us
  waiting for transfers between devices  52.7 us (39%)
  blocking collectives  26.7 us (20%)
  matrix products  21.9 us (16%)
  between operations  14.1 us (11%)
  starting transfers between devices  11 us (8%)
  other arithmetic  4.33 us (3%)
  local copies, waits for them, and re-layouts  1.62 us (1%)
    all_gather x1, waiting for transfers between devices, on_device(): gathered_part = lax.all_gather(grad_z, 'rep', axis=1, tiled=True)  43.8 us
    all_gather x1, blocking collectives, on_device(): all_gather(grad_w, 'blk')  26.7 us
    dot_general x1, matrix products, on_device(): jnp.dot(selector, flat_terms, preferred_element_type=jnp.float32, precisi...  11.3 us
    ppermute x4, starting transfers between devices, from_behind(): return lax.ppermute(value, axis, pairs)  11 us
    dot_general x1, matrix products, on_device(): jnp.einsum('bkij,bfi->bkfj', tiles, grad_hb, preferred_element_type=jnp.f...  9.9 us
    ppermute x4, waiting for transfers between devices, from_behind(): return lax.ppermute(value, axis, pairs)  8.84 us
  transfers between devices with their start and end apart: 5, of which 2 were waited for; matrix products, arithmetic and copies ran while one was open for 3% of the time, Pallas kernels for 0%

profile of v1, /device:TPU:0, one launch (start us, length us, event | category | flops | bytes accessed | tf_op | source)
XLA Modules:
  0.0 132.4 jit_solution(11192166214948981971)
XLA Ops:
  7.2 0.0 copy-start
  7.2 0.0 all-gather.3.cloned.1.call-start
  7.2 1.9 %convert_multiply_fusion = bf16[32,32,128]{2,1,0:T(8,128)(2,1)} fusion(bf16[32,32,128]{2,1,0:T(8,128)(2,1)} %param.7, s32[32,32,128]{2,1,0:T(8,128)} %param.8), kind=kLoop, calls=%fused_computation.19 | loop fusion | flops 262144 | bytes 1048576 | tf_op jit(solution)/shard_map/mul | solution.py:21
  9.1 0.0 all-gather.3.cloned.1.call-update
  9.1 0.8 copy.9
  9.9 0.1 reshape.102
  10.0 0.7 fusion.13
  10.7 0.1 reshape.104
  10.8 43.8 %all-gather.3.cloned.1.call-done = bf16[32,256,128]{2,1,0:T(8,128)(2,1)} async-done(((bf16[32,32,128]{2,1,0:T(8,128)(2,1)}), bf16[32,256,128]{2,1,0:T(8,128)(2,1)}) %all-gather.3.cloned.1.call-update) | async-done | bytes 2097168 | tf_op jit(solution)/shard_map/all_gather | solution.py:22
  54.6 9.9 %fusion.4 = f32[32,32,16,128]{3,1,2,0:T(8,128)} fusion(bf16[32,16,128,128]{3,2,1,0:T(8,128)(2,1)} %param.11, bf16[32,256,128]{2,1,0:T(8,128)(2,1)} %all-gather.3.cloned.1.call-done, bf16[32,256]{1,0:T(8,128)(2,1)} %param.10), kind=kOutput, calls=%fused_computation.6 | convolution fusion | flops 604110848 | bytes 27279360 | tf_op jit(solution)/shard_map/bkij,bfi->bkfj/dot_general | solution.py:35
  64.5 11.3 %fusion = f32[160,4096]{1,0:T(8,128)S(1)} fusion(f32[64,8,32,128]{3,2,1,0:T(8,128)} %bitcast.47, f32[512]{0:T(512)S(1)} %reshape.104, s32[512]{0:T(512)S(1)} %fusion.18), kind=kOutput, calls=%fused_computation | convolution fusion | flops 4026695680 | bytes 11014144 | tf_op jit(solution)/shard_map/dot_general | solution.py:46
  75.9 0.2 slice_bitcast_fusion.4
  76.0 0.1 copy.13
  76.1 0.1 collective-permute-start
  76.2 0.1 copy.15
  76.3 5.4 %collective-permute-start.2 = (f32[32,32,128]{2,1,0:T(8,128)S(1)}, f32[32,32,128]{2,1,0:T(8,128)S(1)}, u32[]{:S(2)}, u32[]{:S(2)}) collective-permute-start(f32[32,32,128]{2,1,0:T(8,128)S(1)} %bitcast.49), channel_id=1, source_target_pairs={{0,120},{8,0},{16,8},{24,16},{32,24},{40,32},{48,40},{56,48},{64,5... | collective-permute-start | bytes 1572872 | tf_op jit(solution)/shard_map/ppermute | solution.py:14
  81.7 0.0 copy-start.1
  81.7 0.1 copy.16
  81.8 0.1 copy.14
  81.9 8.8 %collective-permute-done = f32[32,32,128]{2,1,0:T(8,128)S(1)} collective-permute-done((f32[32,32,128]{2,1,0:T(8,128)S(1)}, f32[32,32,128]{2,1,0:T(8,128)S(1)}, u32[]{:S(2)}, u32[]{:S(2)}) %collective-permute-start) | collective-permute-done | bytes 524320 | tf_op jit(solution)/shard_map/ppermute | solution.py:14
  90.8 0.1 bitcast_add_fusion.1
  90.9 0.1 collective-permute-start.1
  90.9 0.0 collective-permute-done.2
  91.0 0.1 bitcast_add_fusion
  91.0 5.4 %collective-permute-start.3 = (f32[32,32,128]{2,1,0:T(8,128)S(1)}, f32[32,32,128]{2,1,0:T(8,128)S(1)}, u32[]{:S(2)}, u32[]{:S(2)}) collective-permute-start(f32[32,32,128]{2,1,0:T(8,128)S(1)} %bitcast_add_fusion), channel_id=1, source_target_pairs={{0,120},{8,0},{16,8},{24,16},{32,24},{40,32},{48,40},{56,48},{64,5... | collective-permute-start | bytes 1572872 | tf_op jit(solution)/shard_map/ppermute | solution.py:14
  96.4 0.0 copy-done
  96.5 0.0 copy-done.1
  96.5 0.7 convolution_bitcast_fusion
  97.2 0.1 copy.12
  97.3 26.7 %all-gather = f32[512,256]{1,0:T(8,128)S(1)} all-gather(f32[32,256]{1,0:T(8,128)S(1)} %convolution_bitcast_fusion), channel_id=2, replica_groups=mesh['blk'=16,'rep'=8] {'blk'}, dimensions={0}, use_global_device_ids=true | all-gather | bytes 557056 | tf_op jit(solution)/shard_map/all_gather | solution.py:30
  124.0 0.6 broadcast_multiply_fusion
  124.7 0.0 collective-permute-done.1
  124.7 0.0 collective-permute-done.3
  124.7 0.9 fusion.6
  (2 shorter events, 0.1 us)
Async XLA Ops:
  7.2 89.3 %copy-start = (bf16[32,32,128]{2,1,0:T(8,128)(2,1)S(1)}, bf16[32,32,128]{2,1,0:T(8,128)(2,1)}, u32[]{:S(2)}) copy-start(bf16[32,32,128]{2,1,0:T(8,128)(2,1)} %param.9) | copy-start | bytes 786436
  7.2 47.5 %all-gather.3.cloned.1.call-start = ((), (), s32[]{:S(2)}) async-start(), calls=%async_computation | async-start | bytes 2359296 | tf_op jit(solution)/shard_map/all_gather | solution.py:22
  76.1 14.6 %collective-permute-start = (f32[32,32,128]{2,1,0:T(8,128)S(1)}, f32[32,32,128]{2,1,0:T(8,128)S(1)}, u32[]{:S(2)}, u32[]{:S(2)}) collective-permute-start(f32[32,32,128]{2,1,0:T(8,128)S(1)} %bitcast.50), channel_id=1, source_target_pairs={{0,8},{8,16},{16,24},{24,32},{32,40},{40,48},{48,56},{56,64},{64,7... | collective-permute-start | bytes 1572872 | tf_op jit(solution)/shard_map/ppermute | solution.py:14
  76.3 14.6 %collective-permute-start.2 = (f32[32,32,128]{2,1,0:T(8,128)S(1)}, f32[32,32,128]{2,1,0:T(8,128)S(1)}, u32[]{:S(2)}, u32[]{:S(2)}) collective-permute-start(f32[32,32,128]{2,1,0:T(8,128)S(1)} %bitcast.49), channel_id=1, source_target_pairs={{0,120},{8,0},{16,8},{24,16},{32,24},{40,32},{48,40},{56,48},{64,5... | collective-permute-start | bytes 1572872 | tf_op jit(solution)/shard_map/ppermute | solution.py:14
  81.7 14.7 %copy-start.1 = (bf16[32,256,128]{2,1,0:T(8,128)(2,1)S(1)}, bf16[32,256,128]{2,1,0:T(8,128)(2,1)}, u32[]{:S(2)}) copy-start(bf16[32,256,128]{2,1,0:T(8,128)(2,1)} %all-gather.3.cloned.1.call-done) | copy-start | bytes 6291460
  90.9 33.8 %collective-permute-start.1 = (f32[32,32,128]{2,1,0:T(8,128)S(1)}, f32[32,32,128]{2,1,0:T(8,128)S(1)}, u32[]{:S(2)}, u32[]{:S(2)}) collective-permute-start(f32[32,32,128]{2,1,0:T(8,128)S(1)} %bitcast_add_fusion.1), channel_id=1, source_target_pairs={{0,8},{8,16},{16,24},{24,32},{32,40},{40,48},{48,56},{56,64},{64,7... | collective-permute-start | bytes 1572872 | tf_op jit(solution)/shard_map/ppermute | solution.py:14
  91.0 33.6 %collective-permute-start.3 = (f32[32,32,128]{2,1,0:T(8,128)S(1)}, f32[32,32,128]{2,1,0:T(8,128)S(1)}, u32[]{:S(2)}, u32[]{:S(2)}) collective-permute-start(f32[32,32,128]{2,1,0:T(8,128)S(1)} %bitcast_add_fusion), channel_id=1, source_target_pairs={{0,120},{8,0},{16,8},{24,16},{32,24},{40,32},{48,40},{56,48},{64,5... | collective-permute-start | bytes 1572872 | tf_op jit(solution)/shard_map/ppermute | solution.py:14
Sparse Core Ops, SparseCore 0:
  10.2 44.3 all-gather.2
